TPU v7x, 256 devices: a whole 4x4x8 slice. The times are simulated.
256 devices in a mesh: rows: 8 (over y, x_lo), cols: 32 (over z, x_hi, core).
Axes of the slice: x: 4 (x_hi: 2, x_lo: 2; x = x_hi * 2 + x_lo), y: 4, z: 8, core: 2. Of those that a mesh axis runs over, the one named last changes fastest.
Arguments:
- counts: bfloat16 [4096, 262144], P('rows', 'cols'), may hold values from 0 to 12, as said below
- start_a: float32 [4096, 128], P(('rows', 'cols')), may hold values from -0.4 to 0.4
- start_b: float32 [16384, 128], P(('cols', 'rows')), may hold values from -0.4 to 0.4
- start_c: float32 [16, 128], replicated, may hold values from -0.4 to 0.4
Outputs:
- factor_a: float32 [4096, 128], P(('rows', 'cols'))
- factor_b: float32 [16384, 128], P(('cols', 'rows'))
- factor_c: float32 [16, 128], replicated
Inputs may be any that keep to these rules, and one draw needn't show every extreme that they name: counts holds whole numbers.
All inputs are finite; a program needn't handle non-finite values.
Results may differ from a plain program's by a relative error of at most 0.009.
Values may be sent and summed in bfloat16 or wider, within the bound.
No kernel may reach another device: no remote copies, remote signals or barrier semaphores. Data moves between devices by JAX's collectives and lax.ppermute only.
A program may use at most 128 MiB of HBM per device.

v0:
```python
import math
import jax
import jax.numpy as jnp
from jax import lax
from jax.sharding import PartitionSpec as P

ITERS = 2


def local(counts, start_a, start_b, start_c):
    rows_here, flat_width = counts.shape
    depth = start_c.shape[0]
    cols_here = flat_width // depth
    total_i = rows_here * lax.axis_size("rows")
    total_j = cols_here * lax.axis_size("cols")
    rate_a = 0.3 / math.sqrt(total_j * depth)
    rate_b = 0.3 / math.sqrt(total_i * depth)
    rate_c = 0.3 / math.sqrt(total_i * total_j)
    local_a, local_b, shared_c = (start_a, start_b, start_c)
    for iteration in range(ITERS):
        low_a = lax.all_gather(local_a.astype(jnp.bfloat16), "cols", axis=0, tiled=True)
        low_b = lax.all_gather(local_b.astype(jnp.bfloat16), "rows", axis=0, tiled=True)
        low_b_wide = low_b.astype(jnp.float32)
        scaled = (low_b_wide[:, None, :] * shared_c[None, :, :]).astype(jnp.bfloat16)
        scaled = scaled.reshape(cols_here * depth, shared_c.shape[1])
        log_rate = lax.dot_general(
            low_a, scaled, (((1,), (1,)), ((), ())), preferred_element_type=jnp.float32
        )
        residual = (jnp.exp(log_rate) - counts.astype(jnp.float32)).astype(jnp.bfloat16)
        grad_a = jnp.dot(residual, scaled, preferred_element_type=jnp.float32)
        mixed = lax.dot_general(
            residual, low_a, (((0,), (0,)), ((), ())), preferred_element_type=jnp.float32
        )
        mixed = mixed.reshape(cols_here, depth, shared_c.shape[1])
        grad_b = jnp.sum(mixed * shared_c[None, :, :], axis=1)
        grad_c = jnp.sum(mixed * low_b_wide[:, None, :], axis=0)
        summed_a = lax.psum_scatter(grad_a, "cols", scatter_dimension=0, tiled=True)
        summed_b = lax.psum_scatter(grad_b, "rows", scatter_dimension=0, tiled=True)
        local_a = local_a - rate_a * summed_a
        local_b = local_b - rate_b * summed_b
        summed_c = lax.psum(grad_c, ("rows", "cols"))
        shared_c = shared_c - rate_c * summed_c
    return (local_a, local_b, shared_c)


def solution(mesh):
    placed = (P("rows", "cols"), P(("rows", "cols"), None), P(("cols", "rows"), None), P())
    return jax.shard_map(
        local,
        mesh=mesh,
        in_specs=placed,
        out_specs=(P(("rows", "cols"), None), P(("cols", "rows"), None), P()),
        check_vma=False,
    )
```

profile of v0, /device:TPU:32, one launch (start us, length us, event | category | flops | bytes accessed | tf_op | source)
XLA Modules:
  0.0 455.2 jit_solution(1326504930640590621)
XLA Ops:
  7.2 0.0 copy-start.2
  7.2 0.0 copy-start.4
  7.2 0.0 copy-start.5
  7.2 0.0 reduce-scatter.5.cloned.1.call-start
  7.2 12.0 %copy.7 = bf16[512,8192]{0,1:T(8,128)(2,1)} copy(bf16[512,8192]{1,0:T(8,128)(2,1)} %param.4) | data formatting | bytes 16777216 | tf_op args[0]
  19.2 0.0 copy-done.2
  19.2 28.6 %all_gather.12 = bf16[512,128]{1,0:T(8,128)(2,1)S(1)} all-gather(bf16[64,128]{1,0:T(8,128)(2,1)S(1)} %convert_element_type.42), channel_id=1, replica_groups=mesh['rows'=8,'cols'=32] {'rows'}, dimensions={0}, use_global_device_ids=true | all-gather | bytes 147456 | tf_op jit(solution)/shard_map/all_gather | solution.py:22
  47.9 0.0 copy-done.4
  47.9 42.5 %all_gather.13 = bf16[512,128]{1,0:T(8,128)(2,1)S(1)} all-gather(bf16[16,128]{1,0:T(8,128)(2,1)S(1)} %convert_element_type.46), channel_id=1, replica_groups=mesh['rows'=8,'cols'=32] {'cols'}, dimensions={0}, use_global_device_ids=true | all-gather | bytes 135168 | tf_op jit(solution)/shard_map/all_gather | solution.py:21
  90.4 0.0 copy-done.5
  90.4 0.4 multiply_convert_fusion.1
  90.8 5.0 %fusion = bf16[512,8192]{0,1:T(8,128)(2,1)S(1)} fusion(bf16[512,8192]{0,1:T(8,128)(2,1)} %copy.7, bf16[8192,128]{1,0:T(8,128)(2,1)S(1)} %bitcast.22, bf16[512,128]{1,0:T(8,128)(2,1)S(1)} %all_gather.13), kind=kOutput, calls=%fused_computation.2 | convolution fusion | flops 1086324736 | bytes 19005440 | tf_op jit(solution)/shard_map/dot_general | solution.py:26
  95.8 0.0 copy-start
  95.8 3.2 copy-done
  99.0 3.0 fusion.4
  102.1 0.0 reduce-scatter.5.cloned.1.call-update
  102.1 0.0 reduce-scatter.7.cloned.1.call-start
  102.1 8.4 %multiply_reduce_fusion.3 = (f32[512,128]{1,0:T(8,128)}, f32[8192,128]{1,0:T(8,128)}) fusion(f32[16,128]{1,0:T(8,128)S(1)} %copy-done.5, bf16[512,8192]{0,1:T(8,128)(2,1)} %copy-done, bf16[512,128]{1,0:T(8,128)(2,1)S(1)} %all_gather.13), kind=kOutput, calls=%fused_computation.8 | convolution fusion | flops 1075773440 | bytes 12984320 | tf_op jit(solution)/shard_map/dot_general | solution.py:31
  110.5 0.0 reduce-scatter.7.cloned.1.call-update
  110.5 0.0 reduce-scatter.9.cloned.1.call-start
  110.6 2.8 multiply_reduce_fusion.2
  113.4 77.1 %psum.14 = f32[16,128]{1,0:T(8,128)S(1)} all-reduce(f32[16,128]{1,0:T(8,128)S(1)} %multiply_reduce_fusion.2), channel_id=1, replica_groups=mesh['rows'=8,'cols'=32] {'rows','cols'}, use_global_device_ids=true, to_apply=%region_4.0 | all-reduce | flops 2048 | bytes 16384 | tf_op jit(solution)/shard_map/psum | solution.py:41
  190.5 21.8 %reduce-scatter.5.cloned.1.call-done = f32[16,128]{1,0:T(8,128)} async-done(((f32[512,128]{1,0:T(8,128)}), f32[16,128]{1,0:T(8,128)}) %reduce-scatter.5.cloned.1.call-update) | async-done | bytes 8208 | tf_op jit(solution)/shard_map/reduce_scatter | solution.py:37
  212.3 0.7 fusion.3
  213.0 38.0 %all_gather.14 = bf16[512,128]{1,0:T(8,128)(2,1)S(1)} all-gather(bf16[16,128]{1,0:T(8,128)(2,1)S(1)} %fusion.3), channel_id=1, replica_groups=mesh['rows'=8,'cols'=32] {'cols'}, dimensions={0}, use_global_device_ids=true | all-gather | bytes 135168 | tf_op jit(solution)/shard_map/all_gather | solution.py:21
  251.0 2.8 reduce-scatter.7.cloned.1.call-done
  253.8 0.8 fusion.2
  254.6 28.5 %all_gather.15 = bf16[512,128]{1,0:T(8,128)(2,1)S(1)} all-gather(bf16[64,128]{1,0:T(8,128)(2,1)S(1)} %fusion.2), channel_id=1, replica_groups=mesh['rows'=8,'cols'=32] {'rows'}, dimensions={0}, use_global_device_ids=true | all-gather | bytes 147456 | tf_op jit(solution)/shard_map/all_gather | solution.py:22
  283.1 0.4 multiply_convert_fusion
  283.5 5.0 %fusion.1 = bf16[512,8192]{0,1:T(8,128)(2,1)S(1)} fusion(bf16[512,8192]{0,1:T(8,128)(2,1)} %copy.7, bf16[512,128]{1,0:T(8,128)(2,1)S(1)} %all_gather.14, bf16[8192,128]{1,0:T(8,128)(2,1)S(1)} %bitcast.24), kind=kOutput, calls=%fused_computation.3 | convolution fusion | flops 1086324736 | bytes 19005440 | tf_op jit(solution)/shard_map/dot_general | solution.py:26
  288.5 0.0 copy-start.1
  288.5 3.2 copy-done.1
  291.7 3.1 fusion.5
  294.8 0.0 reduce-scatter.9.cloned.1.call-update
  294.8 0.0 reduce-scatter.11.cloned.1.call-start
  294.9 8.4 %multiply_reduce_fusion.1 = (f32[512,128]{1,0:T(8,128)}, f32[8192,128]{1,0:T(8,128)}) fusion(f32[16,128]{1,0:T(8,128)S(1)} %multiply_subtract_fusion.4, bf16[512,8192]{0,1:T(8,128)(2,1)} %copy-done.1, bf16[512,128]{1,0:T(8,128)(2,1)S(1)} %all_gather.14), kind=kOutput, calls=%fused_computation.5 | convolution fusion | flops 1075773440 | bytes 12984320 | tf_op jit(solution)/shard_map/dot_general | solution.py:31
  303.3 0.0 copy-start.6
  303.3 0.0 copy-start.3
  303.3 0.0 reduce-scatter.11.cloned.1.call-update
  303.3 2.8 multiply_reduce_fusion
  306.1 73.2 %psum.15 = f32[16,128]{1,0:T(8,128)S(1)} all-reduce(f32[16,128]{1,0:T(8,128)S(1)} %multiply_reduce_fusion), channel_id=1, replica_groups=mesh['rows'=8,'cols'=32] {'rows','cols'}, use_global_device_ids=true, to_apply=%region_9.0 | all-reduce | flops 2048 | bytes 16384 | tf_op jit(solution)/shard_map/psum | solution.py:41
  379.4 0.6 multiply_subtract_fusion.2
  380.0 25.9 %reduce-scatter.9.cloned.1.call-done = f32[16,128]{1,0:T(8,128)} async-done(((f32[512,128]{1,0:T(8,128)}), f32[16,128]{1,0:T(8,128)}) %reduce-scatter.9.cloned.1.call-update) | async-done | bytes 8208 | tf_op jit(solution)/shard_map/reduce_scatter | solution.py:37
  405.9 0.0 copy-done.6
  405.9 1.3 multiply_subtract_fusion.3
  407.2 40.1 %reduce-scatter.11.cloned.1.call-done = f32[64,128]{1,0:T(8,128)} async-done(((f32[512,128]{1,0:T(8,128)}), f32[64,128]{1,0:T(8,128)}) %reduce-scatter.11.cloned.1.call-update) | async-done | bytes 32784 | tf_op jit(solution)/shard_map/reduce_scatter | solution.py:38
  447.3 0.0 copy-done.3
  447.3 1.4 multiply_subtract_fusion
  (5 shorter events, 0.0 us)
Async XLA Ops:
  7.2 12.0 %copy-start.2 = (f32[64,128]{1,0:T(8,128)S(1)}, f32[64,128]{1,0:T(8,128)}, u32[]{:S(2)}) copy-start(f32[64,128]{1,0:T(8,128)} %param.6) | copy-start | bytes 98308
  7.2 40.7 %copy-start.4 = (f32[16,128]{1,0:T(8,128)S(1)}, f32[16,128]{1,0:T(8,128)}, u32[]{:S(2)}) copy-start(f32[16,128]{1,0:T(8,128)} %param.5) | copy-start | bytes 24580
  7.2 83.2 %copy-start.5 = (f32[16,128]{1,0:T(8,128)S(1)}, f32[16,128]{1,0:T(8,128)}, u32[]{:S(2)}) copy-start(f32[16,128]{1,0:T(8,128)} %param.7) | copy-start | bytes 24580
  7.2 205.1 %reduce-scatter.5.cloned.1.call-start = ((), (), s32[]{:S(2)}) async-start(), calls=%async_computation.4 | async-start | bytes 270336 | tf_op jit(solution)/shard_map/reduce_scatter | solution.py:37
  95.8 3.2 copy-start
  102.1 151.7 %reduce-scatter.7.cloned.1.call-start = ((), (), s32[]{:S(2)}) async-start(), calls=%async_computation.5 | async-start | bytes 294912 | tf_op jit(solution)/shard_map/reduce_scatter | solution.py:38
  110.5 295.3 %reduce-scatter.9.cloned.1.call-start = ((), (), s32[]{:S(2)}) async-start(), calls=%async_computation.6 | async-start | bytes 270336 | tf_op jit(solution)/shard_map/reduce_scatter | solution.py:37
  288.5 3.2 copy-start.1
  294.8 152.5 %reduce-scatter.11.cloned.1.call-start = ((), (), s32[]{:S(2)}) async-start(), calls=%async_computation.7 | async-start | bytes 294912 | tf_op jit(solution)/shard_map/reduce_scatter | solution.py:38
  303.3 102.6 %copy-start.6 = (f32[16,128]{1,0:T(8,128)S(1)}, f32[16,128]{1,0:T(8,128)}, u32[]{:S(2)}) copy-start(f32[16,128]{1,0:T(8,128)} %reduce-scatter.5.cloned.1.call-done) | copy-start | bytes 24580
  303.3 144.0 %copy-start.3 = (f32[64,128]{1,0:T(8,128)S(1)}, f32[64,128]{1,0:T(8,128)}, u32[]{:S(2)}) copy-start(f32[64,128]{1,0:T(8,128)} %reduce-scatter.7.cloned.1.call-done) | copy-start | bytes 98308
Sparse Core Ops, SparseCore 0:
  102.2 110.0 reduce-scatter.4
  214.8 38.9 reduce-scatter.6
  294.9 110.8 reduce-scatter.8
  408.4 38.8 reduce-scatter.10
where the time goes:
time: 456 us; the launch traced here: 455 us
  blocking collectives  288 us (63%)
  waiting for transfers between devices  90.7 us (20%)
  matrix products  33 us (7%)
  local copies, waits for them, and re-layouts  18.4 us (4%)
  between operations  13.9 us (3%)
  other arithmetic  11.1 us (2%)
    psum x2, blocking collectives, local(): summed_c = lax.psum(grad_c, ('rows', 'cols'))  150 us
    all_gather x2, blocking collectives, local(): lax.all_gather(local_a.astype(jnp.bfloat16), 'cols', axis=0, tiled=True)  80.5 us
    all_gather x2, blocking collectives, local(): lax.all_gather(local_b.astype(jnp.bfloat16), 'rows', axis=0, tiled=True)  57.1 us
    reduce_scatter x2, waiting for transfers between devices, local(): summed_a = lax.psum_scatter(grad_a, 'cols', scatter_dimension=0, tiled=True)  47.7 us
    reduce_scatter x2, waiting for transfers between devices, local(): summed_b = lax.psum_scatter(grad_b, 'rows', scatter_dimension=0, tiled=True)  42.9 us
    unnamed x15, local copies, waits for them, and re-layouts  18.4 us
    dot_general x2, matrix products, local(): lax.dot_general(residual, low_a, (((0,), (0,)), ((), ())), preferred_elem...  16.8 us
    dot_general x2, matrix products, local(): lax.dot_general(low_a, scaled, (((1,), (1,)), ((), ())), preferred_elemen...  10.1 us
  transfers between devices with their start and end apart: 4, of which 4 were waited for; matrix products, arithmetic and copies ran while one was open for 5% of the time, Pallas kernels for 0%

commit v1 on v0

--- a/solution.py
+++ b/solution.py
@@ -38,7 +38,7 @@
         summed_b = lax.psum_scatter(grad_b, "rows", scatter_dimension=0, tiled=True)
         local_a = local_a - rate_a * summed_a
         local_b = local_b - rate_b * summed_b
-        summed_c = lax.psum(grad_c, ("rows", "cols"))
+        summed_c = lax.psum(lax.psum(grad_c, "rows"), "cols")
         shared_c = shared_c - rate_c * summed_c
     return (local_a, local_b, shared_c)
 

time: 456 us -> 456 us (level)
  blocking collectives: 288 us -> 293 us
  waiting for transfers between devices: 90.7 us -> 85.7 us
    reduce_scatter x2, waiting for transfers between devices: 47.7 us -> 42.8 us  [local(): summed_a = lax.psum_scatter(grad_a, 'cols', scatter_dimension=0, tiled=True)]
    psum x2 -> x4, blocking collectives: 150 us -> 155 us  [local(): summed_c = lax.psum(lax.psum(grad_c, 'rows'), 'cols')]
where the time goes in v1:
time: 456 us; the launch traced here: 455 us
  blocking collectives  293 us (64%)
  waiting for transfers between devices  85.7 us (19%)
  matrix products  33 us (7%)
  local copies, waits for them, and re-layouts  18.4 us (4%)
  between operations  13.9 us (3%)
  other arithmetic  11.1 us (2%)
    psum x4, blocking collectives, local(): summed_c = lax.psum(lax.psum(grad_c, 'rows'), 'cols')  155 us
    all_gather x2, blocking collectives, local(): lax.all_gather(local_a.astype(jnp.bfloat16), 'cols', axis=0, tiled=True)  80.6 us
    all_gather x2, blocking collectives, local(): lax.all_gather(local_b.astype(jnp.bfloat16), 'rows', axis=0, tiled=True)  57.1 us
    reduce_scatter x2, waiting for transfers between devices, local(): summed_a = lax.psum_scatter(grad_a, 'cols', scatter_dimension=0, tiled=True)  42.8 us
    reduce_scatter x2, waiting for transfers between devices, local(): summed_b = lax.psum_scatter(grad_b, 'rows', scatter_dimension=0, tiled=True)  42.8 us
    unnamed x15, local copies, waits for them, and re-layouts  18.4 us
    dot_general x2, matrix products, local(): lax.dot_general(residual, low_a, (((0,), (0,)), ((), ())), preferred_elem...  16.8 us
    dot_general x2, matrix products, local(): lax.dot_general(low_a, scaled, (((1,), (1,)), ((), ())), preferred_elemen...  10.1 us
  transfers between devices with their start and end apart: 4, of which 4 were waited for; matrix products, arithmetic and copies ran while one was open for 5% of the time, Pallas kernels for 0%

profile of v1, /device:TPU:32, one launch (start us, length us, event | category | flops | bytes accessed | tf_op | source)
XLA Modules:
  0.0 455.2 jit_solution(10490463855169546024)
XLA Ops:
  7.2 0.0 copy-start.2
  7.2 0.0 copy-start.4
  7.2 0.0 copy-start.5
  7.2 0.0 reduce-scatter.5.cloned.1.call-start
  7.2 12.0 %copy.7 = bf16[512,8192]{0,1:T(8,128)(2,1)} copy(bf16[512,8192]{1,0:T(8,128)(2,1)} %param.4) | data formatting | bytes 16777216 | tf_op args[0]
  19.2 0.0 copy-done.2
  19.2 28.6 %all_gather.12 = bf16[512,128]{1,0:T(8,128)(2,1)S(1)} all-gather(bf16[64,128]{1,0:T(8,128)(2,1)S(1)} %convert_element_type.42), channel_id=1, replica_groups=mesh['rows'=8,'cols'=32] {'rows'}, dimensions={0}, use_global_device_ids=true | all-gather | bytes 147456 | tf_op jit(solution)/shard_map/all_gather | solution.py:22
  47.9 0.0 copy-done.4
  47.9 42.5 %all_gather.13 = bf16[512,128]{1,0:T(8,128)(2,1)S(1)} all-gather(bf16[16,128]{1,0:T(8,128)(2,1)S(1)} %convert_element_type.46), channel_id=1, replica_groups=mesh['rows'=8,'cols'=32] {'cols'}, dimensions={0}, use_global_device_ids=true | all-gather | bytes 135168 | tf_op jit(solution)/shard_map/all_gather | solution.py:21
  90.4 0.0 copy-done.5
  90.4 0.4 multiply_convert_fusion.1
  90.8 5.0 %fusion = bf16[512,8192]{0,1:T(8,128)(2,1)S(1)} fusion(bf16[512,8192]{0,1:T(8,128)(2,1)} %copy.7, bf16[8192,128]{1,0:T(8,128)(2,1)S(1)} %bitcast.22, bf16[512,128]{1,0:T(8,128)(2,1)S(1)} %all_gather.13), kind=kOutput, calls=%fused_computation.2 | convolution fusion | flops 1086324736 | bytes 19005440 | tf_op jit(solution)/shard_map/dot_general | solution.py:26
  95.8 0.0 copy-start
  95.8 3.2 copy-done
  99.0 3.0 fusion.4
  102.1 0.0 reduce-scatter.5.cloned.1.call-update
  102.1 0.0 reduce-scatter.7.cloned.1.call-start
  102.1 8.4 %multiply_reduce_fusion.3 = (f32[512,128]{1,0:T(8,128)}, f32[8192,128]{1,0:T(8,128)}) fusion(f32[16,128]{1,0:T(8,128)S(1)} %copy-done.5, bf16[512,8192]{0,1:T(8,128)(2,1)} %copy-done, bf16[512,128]{1,0:T(8,128)(2,1)S(1)} %all_gather.13), kind=kOutput, calls=%fused_computation.8 | convolution fusion | flops 1075773440 | bytes 12984320 | tf_op jit(solution)/shard_map/dot_general | solution.py:31
  110.5 0.0 reduce-scatter.7.cloned.1.call-update
  110.5 0.0 reduce-scatter.9.cloned.1.call-start
  110.6 2.8 multiply_reduce_fusion.2
  113.4 19.1 %psum.28 = f32[16,128]{1,0:T(8,128)S(1)} all-reduce(f32[16,128]{1,0:T(8,128)S(1)} %multiply_reduce_fusion.2), channel_id=1, replica_groups=mesh['rows'=8,'cols'=32] {'rows'}, use_global_device_ids=true, to_apply=%region_4.0 | all-reduce | flops 2048 | bytes 16384 | tf_op jit(solution)/shard_map/psum | solution.py:41
  132.4 59.9 %psum.29 = f32[16,128]{1,0:T(8,128)S(1)} all-reduce(f32[16,128]{1,0:T(8,128)S(1)} %psum.28), channel_id=1, replica_groups=mesh['rows'=8,'cols'=32] {'cols'}, use_global_device_ids=true, to_apply=%region_5.0 | all-reduce | flops 2048 | bytes 16384 | tf_op jit(solution)/shard_map/psum | solution.py:41
  192.3 20.0 %reduce-scatter.5.cloned.1.call-done = f32[16,128]{1,0:T(8,128)} async-done(((f32[512,128]{1,0:T(8,128)}), f32[16,128]{1,0:T(8,128)}) %reduce-scatter.5.cloned.1.call-update) | async-done | bytes 8208 | tf_op jit(solution)/shard_map/reduce_scatter | solution.py:37
  212.4 0.7 fusion.3
  213.1 38.1 %all_gather.14 = bf16[512,128]{1,0:T(8,128)(2,1)S(1)} all-gather(bf16[16,128]{1,0:T(8,128)(2,1)S(1)} %fusion.3), channel_id=1, replica_groups=mesh['rows'=8,'cols'=32] {'cols'}, dimensions={0}, use_global_device_ids=true | all-gather | bytes 135168 | tf_op jit(solution)/shard_map/all_gather | solution.py:21
  251.2 2.7 reduce-scatter.7.cloned.1.call-done
  253.9 0.8 fusion.2
  254.7 28.5 %all_gather.15 = bf16[512,128]{1,0:T(8,128)(2,1)S(1)} all-gather(bf16[64,128]{1,0:T(8,128)(2,1)S(1)} %fusion.2), channel_id=1, replica_groups=mesh['rows'=8,'cols'=32] {'rows'}, dimensions={0}, use_global_device_ids=true | all-gather | bytes 147456 | tf_op jit(solution)/shard_map/all_gather | solution.py:22
  283.2 0.4 multiply_convert_fusion
  283.5 5.0 %fusion.1 = bf16[512,8192]{0,1:T(8,128)(2,1)S(1)} fusion(bf16[512,8192]{0,1:T(8,128)(2,1)} %copy.7, bf16[512,128]{1,0:T(8,128)(2,1)S(1)} %all_gather.14, bf16[8192,128]{1,0:T(8,128)(2,1)S(1)} %bitcast.24), kind=kOutput, calls=%fused_computation.3 | convolution fusion | flops 1086324736 | bytes 19005440 | tf_op jit(solution)/shard_map/dot_general | solution.py:26
  288.6 0.0 copy-start.1
  288.6 3.2 copy-done.1
  291.8 3.1 fusion.5
  294.9 0.0 reduce-scatter.9.cloned.1.call-update
  294.9 0.0 reduce-scatter.11.cloned.1.call-start
  294.9 8.4 %multiply_reduce_fusion.1 = (f32[512,128]{1,0:T(8,128)}, f32[8192,128]{1,0:T(8,128)}) fusion(f32[16,128]{1,0:T(8,128)S(1)} %multiply_subtract_fusion.4, bf16[512,8192]{0,1:T(8,128)(2,1)} %copy-done.1, bf16[512,128]{1,0:T(8,128)(2,1)S(1)} %all_gather.14), kind=kOutput, calls=%fused_computation.5 | convolution fusion | flops 1075773440 | bytes 12984320 | tf_op jit(solution)/shard_map/dot_general | solution.py:31
  303.4 0.0 reduce-scatter.11.cloned.1.call-update
  303.4 2.8 multiply_reduce_fusion
  306.2 16.8 %psum.30 = f32[16,128]{1,0:T(8,128)S(1)} all-reduce(f32[16,128]{1,0:T(8,128)S(1)} %multiply_reduce_fusion), channel_id=1, replica_groups=mesh['rows'=8,'cols'=32] {'rows'}, use_global_device_ids=true, to_apply=%region_10.0 | all-reduce | flops 2048 | bytes 16384 | tf_op jit(solution)/shard_map/psum | solution.py:41
  322.9 59.6 %psum.31 = f32[16,128]{1,0:T(8,128)S(1)} all-reduce(f32[16,128]{1,0:T(8,128)S(1)} %psum.30), channel_id=1, replica_groups=mesh['rows'=8,'cols'=32] {'cols'}, use_global_device_ids=true, to_apply=%region_11.0 | all-reduce | flops 2048 | bytes 16384 | tf_op jit(solution)/shard_map/psum | solution.py:41
  382.5 0.6 multiply_subtract_fusion.2
  383.1 22.8 %reduce-scatter.9.cloned.1.call-done = f32[16,128]{1,0:T(8,128)} async-done(((f32[512,128]{1,0:T(8,128)}), f32[16,128]{1,0:T(8,128)}) %reduce-scatter.9.cloned.1.call-update) | async-done | bytes 8208 | tf_op jit(solution)/shard_map/reduce_scatter | solution.py:37
  405.9 0.0 copy-done.6
  405.9 1.3 multiply_subtract_fusion.3
  407.2 40.1 %reduce-scatter.11.cloned.1.call-done = f32[64,128]{1,0:T(8,128)} async-done(((f32[512,128]{1,0:T(8,128)}), f32[64,128]{1,0:T(8,128)}) %reduce-scatter.11.cloned.1.call-update) | async-done | bytes 32784 | tf_op jit(solution)/shard_map/reduce_scatter | solution.py:38
  447.3 0.0 copy-done.3
  447.3 1.4 multiply_subtract_fusion
  (7 shorter events, 0.1 us)
Async XLA Ops:
  7.2 12.0 %copy-start.2 = (f32[64,128]{1,0:T(8,128)S(1)}, f32[64,128]{1,0:T(8,128)}, u32[]{:S(2)}) copy-start(f32[64,128]{1,0:T(8,128)} %param.6) | copy-start | bytes 98308
  7.2 40.7 %copy-start.4 = (f32[16,128]{1,0:T(8,128)S(1)}, f32[16,128]{1,0:T(8,128)}, u32[]{:S(2)}) copy-start(f32[16,128]{1,0:T(8,128)} %param.5) | copy-start | bytes 24580
  7.2 83.2 %copy-start.5 = (f32[16,128]{1,0:T(8,128)S(1)}, f32[16,128]{1,0:T(8,128)}, u32[]{:S(2)}) copy-start(f32[16,128]{1,0:T(8,128)} %param.7) | copy-start | bytes 24580
  7.2 205.2 %reduce-scatter.5.cloned.1.call-start = ((), (), s32[]{:S(2)}) async-start(), calls=%async_computation.4 | async-start | bytes 270336 | tf_op jit(solution)/shard_map/reduce_scatter | solution.py:37
  95.8 3.2 copy-start
  102.1 151.8 %reduce-scatter.7.cloned.1.call-start = ((), (), s32[]{:S(2)}) async-start(), calls=%async_computation.5 | async-start | bytes 294912 | tf_op jit(solution)/shard_map/reduce_scatter | solution.py:38
  110.5 295.4 %reduce-scatter.9.cloned.1.call-start = ((), (), s32[]{:S(2)}) async-start(), calls=%async_computation.6 | async-start | bytes 270336 | tf_op jit(solution)/shard_map/reduce_scatter | solution.py:37
  288.6 3.2 copy-start.1
  294.9 152.4 %reduce-scatter.11.cloned.1.call-start = ((), (), s32[]{:S(2)}) async-start(), calls=%async_computation.7 | async-start | bytes 294912 | tf_op jit(solution)/shard_map/reduce_scatter | solution.py:38
  303.4 102.5 %copy-start.6 = (f32[16,128]{1,0:T(8,128)S(1)}, f32[16,128]{1,0:T(8,128)}, u32[]{:S(2)}) copy-start(f32[16,128]{1,0:T(8,128)} %reduce-scatter.5.cloned.1.call-done) | copy-start | bytes 24580
  303.4 143.9 %copy-start.3 = (f32[64,128]{1,0:T(8,128)S(1)}, f32[64,128]{1,0:T(8,128)}, u32[]{:S(2)}) copy-start(f32[64,128]{1,0:T(8,128)} %reduce-scatter.7.cloned.1.call-done) | copy-start | bytes 98308
Sparse Core Ops, SparseCore 0:
  102.2 110.0 reduce-scatter.4
  214.9 38.9 reduce-scatter.6
  295.0 110.8 reduce-scatter.8
  408.4 38.8 reduce-scatter.10
